TPU v7x, 128 devices: a whole 4x4x4 slice. The times are simulated.
128 devices in a mesh: grid: 32 (over y, z, core), elem: 4 (over x).
Axes of the slice: x: 4, y: 4, z: 4, core: 2. Of those that a mesh axis runs over, the one named last changes fastest.
Arguments:
- jacobians: bfloat16 [4096, 320, 320], P(('grid', 'elem'))
- residual: bfloat16 [4096, 320], P(('grid', 'elem')), may hold values from -6 to 6
- owner_map: int32 [4096], P(('grid', 'elem')), may hold values from -1 to 31, as said below
- owner_slot: int32 [2048], P(('grid', 'elem')), may hold values from 0 to 31, as said below
- face_coupling: bfloat16 [320, 1920], replicated, may hold values from -0.109375 to 0.109375
- neighbours: int32 [6, 4096], P(None, ('grid', 'elem')), may hold values from -1 to 127, as said below
- donors: int32 [8192], P(('grid', 'elem')), may hold values from -1 to 31, as said below
- receptors: int32 [3, 16384], P(None, ('grid', 'elem')), may hold values from 0 to 63, as said below
- receptor_coords: float32 [3, 16384], P(None, ('grid', 'elem')), may hold values from -1 to 1
Outputs:
- precond: bfloat16 [2048, 320, 320], P(('grid', 'elem'))
- update: float32 [4096, 320], P(('grid', 'elem'))
Inputs may be any that keep to these rules, and one draw needn't show every extreme that they name: `owner_map`: entry -1 marks an empty slot; a live entry g' + k sends the element to the device of grid index g' with the same elem index, as the k-th of at most 1 elements from this device to that one; a device uses each entry value at most once. A quarter of the grids, drawn from the seed, fill all 32 slots of their devices and send exactly 1 elements to every owner; the other grids' devices hold about a third as many. `owner_slot`: each device lists 16 distinct grid indices g, exactly those from whose device with the same elem index a live element arrives. `neighbours`: entry [f, n] of a live element names its neighbour across face f as e * 32 + s, slot s of the device with elem index e and the same grid index, or -1 at a boundary; the neighbour is live and names n back across face f xor 1. Empty slots hold -1. `donors`: on a device of grid index h, entry g * 2 + k names a live slot of that device, the k-th donor element for grid g; entries with g = h are -1. `receptors`: row 0 is a donor row h * 2 + k with h not the device's own grid index; row 1 a live slot of the device; row 2 a solution point index below 64.
All inputs are finite; a program needn't handle non-finite values.
Results may differ from a plain program's by a relative error of at most 0.0058.
Values may be sent and summed in bfloat16 or wider, within the bound.
A program may use at most 192 MiB of HBM per device.

v0:
```python
import jax
import jax.numpy as jnp
from jax import lax
from jax.sharding import PartitionSpec as P

VARS = 5
NODES = 4
NS_ITERS = 3


def basis_weights(receptor_coords):
    node_places = -jnp.cos(jnp.pi * jnp.arange(NODES, dtype=jnp.float32) / (NODES - 1))
    diagonal_mask = jnp.eye(NODES, dtype=bool)
    node_gaps = jnp.where(
        diagonal_mask, jnp.float32(1.0), node_places[:, None] - node_places[None, :]
    )
    denominator = jnp.prod(node_gaps, axis=1)
    factors = []
    for direction in range(3):
        position = receptor_coords[direction]
        offsets = position[None, :] - node_places[:, None]
        numerator = jnp.prod(
            jnp.where(diagonal_mask[:, :, None], jnp.float32(1.0), offsets[None, :, :]), axis=1
        )
        factors.append(numerator / denominator[:, None])
    table = (
        factors[0][:, None, None, :] * factors[1][None, :, None, :] * factors[2][None, None, :, :]
    )
    return table.reshape(NODES**3, -1)


def invert_blocks(blocks):
    matrix = blocks.astype(jnp.float32)
    diagonal = jnp.diagonal(matrix, axis1=-2, axis2=-1)
    identity = jnp.eye(matrix.shape[-1], dtype=jnp.float32)
    approx = identity[None] / diagonal[:, None, :]
    for iteration in range(NS_ITERS):
        product = jnp.einsum("oij,ojk->oik", matrix, approx, precision=lax.Precision.HIGHEST)
        approx = 2.0 * approx - jnp.einsum(
            "oij,ojk->oik", approx, product, precision=lax.Precision.HIGHEST
        )
    return approx.astype(jnp.bfloat16)


def apply_blocks(block_set, vectors):
    return jnp.einsum("obc,oc->ob", block_set, vectors, preferred_element_type=jnp.float32)


def shards(
    jacobians,
    residual,
    owner_map,
    owner_slot,
    face_coupling,
    neighbours,
    donors,
    receptors,
    receptor_coords,
):
    slot_count = jacobians.shape[0]
    width = jacobians.shape[1]
    owned_count = owner_slot.shape[0]
    point_count = width // VARS
    group_slots = lax.axis_size("elem") * slot_count
    live_slots = owner_map >= 0
    slot_iota = jnp.arange(slot_count, dtype=jnp.int32)
    send_target = jnp.where(live_slots, owner_map, slot_count)
    slot_for_send = (
        jnp.zeros((slot_count + 1,), jnp.int32).at[send_target].set(slot_iota)[:slot_count]
    )
    owned_for_send = (
        jnp.zeros((slot_count,), jnp.int32)
        .at[owner_slot]
        .set(jnp.arange(owned_count, dtype=jnp.int32))
    )
    back_index = jnp.where(live_slots, owner_map, 0)
    outgoing = jnp.take(jacobians, slot_for_send, axis=0)
    arrived_blocks = lax.all_to_all(outgoing, "grid", split_axis=0, concat_axis=0, tiled=True)
    precond = invert_blocks(jnp.take(arrived_blocks, owner_slot, axis=0))
    returned = lax.all_to_all(
        jnp.take(precond, owned_for_send, axis=0), "grid", split_axis=0, concat_axis=0, tiled=True
    )
    native_blocks = jnp.take(returned, back_index, axis=0)
    first_guess = apply_blocks(native_blocks, residual).astype(jnp.bfloat16)
    face_terms = jnp.dot(first_guess, face_coupling, preferred_element_type=jnp.float32).astype(
        jnp.bfloat16
    )
    everyone = lax.all_gather(face_terms, "elem", axis=0, tiled=True).reshape(group_slots, 6, width)
    face_sum = jnp.zeros((slot_count, width), jnp.float32)
    for face_index in range(6):
        neighbour = neighbours[face_index]
        face_rows = everyone[jnp.clip(neighbour, 0), face_index ^ 1].astype(jnp.float32)
        face_sum = face_sum + jnp.where((neighbour >= 0)[:, None], face_rows, jnp.float32(0.0))
    sent_rows = jnp.take(first_guess, jnp.clip(donors, 0), axis=0)
    donor_values = lax.all_to_all(sent_rows, "grid", split_axis=0, concat_axis=0, tiled=True)
    picked = (
        jnp.take(donor_values, receptors[0], axis=0)
        .astype(jnp.float32)
        .reshape(-1, VARS, point_count)
    )
    fringe_values = jnp.einsum(
        "rvp,pr->rv", picked, basis_weights(receptor_coords), precision=lax.Precision.HIGHEST
    )
    flat_index = (
        (receptors[1] * width)[:, None]
        + jnp.arange(VARS, dtype=jnp.int32)[None, :] * point_count
        + receptors[2][:, None]
    )
    fringe = (
        jnp.zeros((slot_count * width,), jnp.float32)
        .at[flat_index.reshape(-1)]
        .add(fringe_values.reshape(-1))
        .reshape(slot_count, width)
    )
    sweep_rhs = (residual.astype(jnp.float32) - face_sum + fringe).astype(jnp.bfloat16)
    update = apply_blocks(native_blocks, sweep_rhs)
    update = jnp.where(live_slots[:, None], update, jnp.float32(0.0))
    return (precond, update)


def solution(mesh):
    in_specs = (
        P(("grid", "elem"), None, None),
        P(("grid", "elem"), None),
        P(("grid", "elem")),
        P(("grid", "elem")),
        P(),
        P(None, ("grid", "elem")),
        P(("grid", "elem")),
        P(None, ("grid", "elem")),
        P(None, ("grid", "elem")),
    )
    out_specs = (P(("grid", "elem"), None, None), P(("grid", "elem"), None))
    return jax.shard_map(shards, mesh=mesh, in_specs=in_specs, out_specs=out_specs, check_vma=False)
```

profile of v0, /device:TPU:10, one launch (start us, length us, event | category | flops | bytes accessed | tf_op | source)
XLA Modules:
  0.0 473.9 jit_solution(18328046091139376310)
XLA Ops:
  0.6 0.0 copy-start
  0.6 0.8 compare_select_fusion.6
  1.4 0.7 scatter_custom_fusion
  2.1 8.4 %gather_fusion.11 = bf16[32,320,320]{2,1,0:T(8,128)(2,1)} fusion(bf16[32,320,320]{2,1,0:T(8,128)(2,1)} %param.11, s32[1024]{0:T(1024)S(1)} %pad_clamp_fusion.5), kind=kCustom, calls=%fused_computation.clone | custom fusion | bytes 13107328 | tf_op jit(solution)/shard_map/jit(_take)/gather | solution.py:77
  10.5 7.3 %broadcast_select_fusion.1 = bf16[32,320,320]{2,1,0:T(8,128)(2,1)} fusion(bf16[32,320,320]{2,1,0:T(8,128)(2,1)} %gather_fusion.11, pred[32]{0:T(512)(128)(4,1)S(1)} %get-tuple-element.8), kind=kLoop, calls=%fused_computation.20 | loop fusion | flops 3276800 | bytes 13107232 | tf_op jit(solution)/shard_map/jit(_take)/select_n | solution.py:77
  17.9 8.7 %all-to-all-start = ((bf16[32,320,320]{2,1,0:T(8,128)(2,1)}), bf16[32,320,320]{2,1,0:T(8,128)(2,1)}, u32[]{:S(2)}, u32[]{:S(2)}) async-start(bf16[32,320,320]{2,1,0:T(8,128)(2,1)} %broadcast_select_fusion.1), calls=%async_computation | async-start | bytes 15728640 | tf_op jit(solution)/shard_map/all_to_all | solution.py:78
  26.6 0.0 copy-done.7
  26.7 0.6 scatter_custom_fusion.1
  27.4 95.7 %all-to-all-done = bf16[32,320,320]{2,1,0:T(8,128)(2,1)} async-done(((bf16[32,320,320]{2,1,0:T(8,128)(2,1)}), bf16[32,320,320]{2,1,0:T(8,128)(2,1)}, u32[]{:S(2)}, u32[]{:S(2)}) %all-to-all-start) | async-done | bytes 6553632 | tf_op jit(solution)/shard_map/all_to_all | solution.py:78
  123.1 6.3 %gather_fusion = bf16[16,320,320]{2,1,0:T(8,128)(2,1)} fusion(bf16[32,320,320]{2,1,0:T(8,128)(2,1)} %all-to-all-done, s32[1024]{0:T(1024)S(1)} %pad_clamp_fusion.4), kind=kCustom, calls=%fused_computation.2 | custom fusion | bytes 6553664 | tf_op jit(solution)/shard_map/jit(_take)/gather | solution.py:79
  129.3 5.8 %fusion.28 = f32[16,320,320]{2,1,0:T(8,128)} fusion(bf16[16,320,320]{2,1,0:T(8,128)(2,1)} %gather_fusion, pred[16]{0:T(512)(128)(4,1)S(1)} %compare_and_fusion.4), kind=kLoop, calls=%fused_computation.114 | loop fusion | flops 3276800 | bytes 9830416 | tf_op jit(solution)/shard_map/convert_element_type | solution.py:33
  135.2 25.7 %copy.28 = f32[16,320,320]{0,2,1:T(8,128)} copy(f32[16,320,320]{2,1,0:T(8,128)} %fusion.28) | data formatting | bytes 13107200 | tf_op jit(solution)/shard_map/convert_element_type | solution.py:33
  160.8 10.9 %gather_fusion.1 = f32[320,16]{1,0:T(8,128)S(1)} fusion(f32[16,320,320]{0,2,1:T(8,128)} %copy.28, s32[320]{0:T(512)S(1)} %or_reduce_fusion), kind=kCustom, calls=%fused_computation.3 | custom fusion | bytes 43520 | tf_op jit(solution)/shard_map/jit(diagonal)/gather | solution.py:34
  171.8 0.1 copy.29
  171.8 9.9 %fusion.2 = f32[16,320,320]{2,1,0:T(8,128)S(1)} fusion(f32[16,320]{1,0:T(8,128)S(1)} %copy.29, f32[320,320]{1,0:T(8,128)S(1)} %fusion.11, bf16[16,320,320]{2,1,0:T(8,128)(2,1)} %gather_fusion, pred[16]{0:T(512)(128)(4,1)S(1)} %compare_and_fusion.4), kind=kOutput, calls=%fused_computation.24 | convolution fusion | flops 6294732800 | bytes 10260496 | tf_op jit(solution)/shard_map/oij,ojk->oik/dot_general | solution.py:38
  181.7 0.0 copy-start.1
  181.7 15.6 %fusion = f32[16,320,320]{2,1,0:T(8,128)S(1)} fusion(f32[16,320,320]{2,1,0:T(8,128)S(1)} %fusion.2, f32[16,320]{1,0:T(8,128)S(1)} %copy.29, f32[320,320]{1,0:T(8,128)S(1)} %fusion.11), kind=kOutput, calls=%fused_computation.22 | convolution fusion | flops 6293094400 | bytes 13537280 | tf_op jit(solution)/shard_map/oij,ojk->oik/dot_general | solution.py:39
  197.3 0.0 copy-start.9
  197.3 3.2 copy-done.9
  200.5 10.3 %fusion.10 = f32[16,320,320]{2,1,0:T(8,128)} fusion(f32[16,320,320]{2,1,0:T(8,128)S(1)} %fusion, f32[16,320]{1,0:T(8,128)S(1)} %copy.29, f32[320,320]{1,0:T(8,128)S(1)} %fusion.11, bf16[16,320,320]{2,1,0:T(8,128)(2,1)S(1)} %copy-done.1, pred[16]{0:T(512)(128)(4,1)S(1)} %compare_and_fusion.4), kind=kOutput, calls=%fused_computation.34 | convolution fusion | flops 6298009600 | bytes 16814096 | tf_op jit(solution)/shard_map/oij,ojk->oik/dot_general | solution.py:38
  210.8 23.3 %multiply_subtract_fusion = f32[16,320,320]{2,1,0:T(8,128)S(1)} fusion(f32[16,320,320]{2,1,0:T(8,128)} %fusion.10, f32[16,320,320]{2,1,0:T(8,128)} %copy-done.9, f32[16,320]{1,0:T(8,128)S(1)} %copy.29, f32[320,320]{1,0:T(8,128)S(1)} %fusion.11), kind=kOutput, calls=%fused_computation.17 | convolution fusion | flops 6304563200 | bytes 20090880 | tf_op jit(solution)/shard_map/oij,ojk->oik/dot_general | solution.py:39
  234.1 10.2 %fusion.27 = f32[16,320,320]{2,1,0:T(8,128)} fusion(f32[16,320,320]{2,1,0:T(8,128)S(1)} %multiply_subtract_fusion, bf16[16,320,320]{2,1,0:T(8,128)(2,1)S(1)} %copy-done.1, pred[16]{0:T(512)(128)(4,1)S(1)} %compare_and_fusion.4), kind=kOutput, calls=%fused_computation.113 | convolution fusion | flops 6293094400 | bytes 16384016 | tf_op jit(solution)/shard_map/oij,ojk->oik/dot_general | solution.py:38
  244.3 18.1 %subtract_convert_fusion = bf16[16,320,320]{2,1,0:T(8,128)(2,1)} fusion(f32[16,320,320]{2,1,0:T(8,128)S(1)} %multiply_subtract_fusion, f32[16,320,320]{2,1,0:T(8,128)} %fusion.27), kind=kOutput, calls=%fused_computation.16 | convolution fusion | flops 6296371200 | bytes 16384000 | tf_op jit(solution)/shard_map/oij,ojk->oik/dot_general | solution.py:39
  262.4 7.2 %gather_fusion.2 = bf16[32,320,320]{2,1,0:T(8,128)(2,1)} fusion(bf16[16,320,320]{2,1,0:T(8,128)(2,1)} %subtract_convert_fusion, s32[1024]{0:T(1024)S(1)} %pad_clamp_fusion.3), kind=kCustom, calls=%fused_computation.4 | custom fusion | bytes 13107328 | tf_op jit(solution)/shard_map/jit(_take)/gather | solution.py:81
  269.6 7.3 %broadcast_select_fusion.2 = bf16[32,320,320]{2,1,0:T(8,128)(2,1)} fusion(bf16[32,320,320]{2,1,0:T(8,128)(2,1)} %gather_fusion.2, pred[32]{0:T(512)(128)(4,1)S(1)} %compare_and_fusion.3), kind=kLoop, calls=%fused_computation.21 | loop fusion | flops 3276800 | bytes 13107232 | tf_op jit(solution)/shard_map/jit(_take)/select_n | solution.py:81
  276.9 0.0 copy-start.3
  277.0 27.1 %all-to-all-start.1 = ((bf16[32,320,320]{2,1,0:T(8,128)(2,1)}), bf16[32,320,320]{2,1,0:T(8,128)(2,1)}, u32[]{:S(2)}, u32[]{:S(2)}) async-start(bf16[32,320,320]{2,1,0:T(8,128)(2,1)} %broadcast_select_fusion.2), calls=%async_computation.1 | async-start | bytes 15728640 | tf_op jit(solution)/shard_map/all_to_all | solution.py:80
  304.1 0.0 copy-done.8
  304.1 0.1 broadcast_in_dim.230
  304.3 0.1 add_add_fusion
  304.4 0.2 add.164
  304.8 0.2 select_reduce_fusion.3
  305.0 0.1 broadcast_subtract_fusion.1
  305.0 0.1 select_reduce_fusion.2
  305.1 0.0 copy-done.3
  305.2 0.1 broadcast_divide_fusion.2
  305.3 0.0 copy-start.2
  305.3 95.1 %all-to-all-done.1 = bf16[32,320,320]{2,1,0:T(8,128)(2,1)} async-done(((bf16[32,320,320]{2,1,0:T(8,128)(2,1)}), bf16[32,320,320]{2,1,0:T(8,128)(2,1)}, u32[]{:S(2)}, u32[]{:S(2)}) %all-to-all-start.1) | async-done | bytes 6553632 | tf_op jit(solution)/shard_map/all_to_all | solution.py:80
  400.4 8.4 %gather_fusion.12 = bf16[32,320,320]{2,1,0:T(8,128)(2,1)} fusion(bf16[32,320,320]{2,1,0:T(8,128)(2,1)} %all-to-all-done.1, s32[1024]{0:T(1024)S(1)} %pad_clamp_fusion.2), kind=kCustom, calls=%fused_computation.1.clone | custom fusion | bytes 13107328 | tf_op jit(solution)/shard_map/jit(_take)/gather | solution.py:83
  408.8 0.0 copy-done.2
  408.8 5.6 %fusion.9 = bf16[32,1,320]{2,1,0:T(2,128)(2,1)S(1)} fusion(bf16[32,320,320]{2,1,0:T(8,128)(2,1)} %gather_fusion.12, pred[32]{0:T(512)(128)(4,1)S(1)} %get-tuple-element.6, bf16[32,320,1]{1,0,2:T(8,128)(2,1)S(1)} %bitcast.69), kind=kOutput, calls=%fused_computation.32 | convolution fusion | flops 9830400 | bytes 6594592 | tf_op jit(solution)/shard_map/obc,oc->ob/dot_general | solution.py:46
  414.4 0.3 convolution_convert_fusion
  414.7 0.7 gather_fusion.9
  415.5 0.7 broadcast_select_fusion.6
  416.2 26.4 %all-to-all-start.2 = ((bf16[32,2,320]{2,1,0:T(2,128)(2,1)}), bf16[32,2,320]{2,1,0:T(2,128)(2,1)S(1)}, u32[]{:S(2)}, u32[]{:S(2)}) async-start(bf16[32,2,320]{2,1,0:T(2,128)(2,1)} %broadcast_select_fusion.6), calls=%async_computation.2 | async-start | bytes 98304 | tf_op jit(solution)/shard_map/all_to_all | solution.py:95
  442.6 13.2 %all_gather.3 = bf16[128,1920]{1,0:T(8,128)(2,1)S(1)} all-gather(bf16[32,1920]{1,0:T(8,128)(2,1)S(1)} %convolution_convert_fusion), channel_id=1, replica_groups=mesh['grid'=32,'elem'=4] {'elem'}, dimensions={0}, use_global_device_ids=true | all-gather | bytes 614400 | tf_op jit(solution)/shard_map/all_gather | solution.py:88
  455.8 0.3 copy.30
  456.1 0.3 copy.31
  456.4 0.7 gather_fusion.8
  457.2 0.7 gather_fusion.3
  457.9 0.7 gather_fusion.4
  458.6 0.7 gather_fusion.5
  459.3 0.7 gather_fusion.6
  460.0 0.7 gather_fusion.7
  460.7 0.0 all-to-all-done.2
  460.8 0.9 gather_fusion.10
  461.6 0.1 copy.37
  461.8 0.1 copy.46
  461.9 0.2 reshape.527
  462.1 5.1 %scatter_custom_fusion.2 = f32[10240]{0:T(1024)S(1)} fusion(s32[640]{0:T(1024)S(1)} %fusion.17, f32[640]{0:T(1024)S(1)} %reshape.527, f32[]{:T(128)} %constant.77.clone.1), kind=kCustom, calls=%fused_computation.46 | custom fusion | flops 640 | bytes 40964 | tf_op jit(solution)/shard_map/scatter-add | solution.py:112
  467.3 0.1 reshape.416
  467.3 0.1 fusion.14
  467.5 5.6 %fusion.8 = f32[32,1,320]{2,1,0:T(1,128)S(1)} fusion(bf16[32,320,320]{2,1,0:T(8,128)(2,1)} %gather_fusion.12, pred[32]{0:T(512)(128)(4,1)S(1)} %get-tuple-element.6, bf16[32,320,1]{1,0,2:T(8,128)(2,1)S(1)} %fusion.14), kind=kOutput, calls=%fused_computation.31 | convolution fusion | flops 9830400 | bytes 6615072 | tf_op jit(solution)/shard_map/obc,oc->ob/dot_general | solution.py:46
  473.0 0.7 bitcast_select_fusion
  (44 shorter events, 0.4 us)
Async XLA Ops:
  0.6 413.8 %copy-start = (bf16[320,1920]{1,0:T(8,128)(2,1)S(1)}, bf16[320,1920]{1,0:T(8,128)(2,1)}, u32[]{:S(2)}) copy-start(bf16[320,1920]{1,0:T(8,128)(2,1)} %param.15) | copy-start | bytes 3686404
  17.9 8.7 %copy-start.7 = (s32[16]{0:T(128)S(1)}, s32[16]{0:T(128)}, u32[]{:S(2)}) copy-start(s32[16]{0:T(128)} %param.14) | copy-start | bytes 196
  17.9 105.2 %all-to-all-start = ((bf16[32,320,320]{2,1,0:T(8,128)(2,1)}), bf16[32,320,320]{2,1,0:T(8,128)(2,1)}, u32[]{:S(2)}, u32[]{:S(2)}) async-start(bf16[32,320,320]{2,1,0:T(8,128)(2,1)} %broadcast_select_fusion.1), calls=%async_computation | async-start | bytes 15728640 | tf_op jit(solution)/shard_map/all_to_all | solution.py:78
  181.7 18.7 %copy-start.1 = (bf16[16,320,320]{2,1,0:T(8,128)(2,1)S(1)}, bf16[16,320,320]{2,1,0:T(8,128)(2,1)}, u32[]{:S(2)}) copy-start(bf16[16,320,320]{2,1,0:T(8,128)(2,1)} %gather_fusion) | copy-start | bytes 9830404
  197.3 3.2 copy-start.9
  276.9 27.2 %copy-start.8 = (s32[64]{0:T(128)S(1)}, s32[64]{0:T(128)}, u32[]{:S(2)}) copy-start(s32[64]{0:T(128)} %param.17) | copy-start | bytes 772
  276.9 27.3 %copy-start.5 = (s32[3,128]{1,0:T(4,128)S(1)}, s32[3,128]{1,0:T(4,128)}, u32[]{:S(2)}) copy-start(s32[3,128]{1,0:T(4,128)} %param.18) | copy-start | bytes 4612
  276.9 27.7 %copy-start.6 = (s32[32]{0:T(128)S(1)}, s32[32]{0:T(128)}, u32[]{:S(2)}) copy-start(s32[32]{0:T(128)} %param.13) | copy-start | bytes 388
  276.9 28.0 %copy-start.4 = (f32[3,128]{1,0:T(4,128)S(1)}, f32[3,128]{1,0:T(4,128)}, u32[]{:S(2)}) copy-start(f32[3,128]{1,0:T(4,128)} %param.19) | copy-start | bytes 4612
  276.9 28.2 %copy-start.3 = (s32[6,32]{1,0:T(8,128)S(1)}, s32[6,32]{1,0:T(8,128)}, u32[]{:S(2)}) copy-start(s32[6,32]{1,0:T(8,128)} %param.16) | copy-start | bytes 2308
  277.0 123.4 %all-to-all-start.1 = ((bf16[32,320,320]{2,1,0:T(8,128)(2,1)}), bf16[32,320,320]{2,1,0:T(8,128)(2,1)}, u32[]{:S(2)}, u32[]{:S(2)}) async-start(bf16[32,320,320]{2,1,0:T(8,128)(2,1)} %broadcast_select_fusion.2), calls=%async_computation.1 | async-start | bytes 15728640 | tf_op jit(solution)/shard_map/all_to_all | solution.py:80
  305.3 103.5 %copy-start.2 = (bf16[32,320]{1,0:T(8,128)(2,1)S(1)}, bf16[32,320]{1,0:T(8,128)(2,1)}, u32[]{:S(2)}) copy-start(bf16[32,320]{1,0:T(8,128)(2,1)} %param.12) | copy-start | bytes 61444
  416.2 44.5 %all-to-all-start.2 = ((bf16[32,2,320]{2,1,0:T(2,128)(2,1)}), bf16[32,2,320]{2,1,0:T(2,128)(2,1)S(1)}, u32[]{:S(2)}, u32[]{:S(2)}) async-start(bf16[32,2,320]{2,1,0:T(2,128)(2,1)} %broadcast_select_fusion.6), calls=%async_computation.2 | async-start | bytes 98304 | tf_op jit(solution)/shard_map/all_to_all | solution.py:95
where the time goes:
time: 483 us; the launch traced here: 474 us
  waiting for transfers between devices  191 us (40%)
  matrix products  98.8 us (20%)
  local copies, waits for them, and re-layouts  78.8 us (16%)
  starting transfers between devices  62.3 us (13%)
  other arithmetic  28.8 us (6%)
  blocking collectives  13.2 us (3%)
    all_to_all x1, waiting for transfers between devices, shards(): lax.all_to_all(outgoing, 'grid', split_axis=0, concat_axis=0, tiled=True)  95.7 us
    all_to_all x1, waiting for transfers between devices, shards(): lax.all_to_all(jnp.take(precond, owned_for_send, axis=0), 'grid', split_a...  95.1 us
    dot_general x3, matrix products, invert_blocks(): jnp.einsum('oij,ojk->oik', approx, product, precision=lax.Precision.HIGHEST)  57 us
    dot_general x3, matrix products, invert_blocks(): jnp.einsum('oij,ojk->oik', matrix, approx, precision=lax.Precision.HIGHEST)  30.4 us
    all_to_all x1, starting transfers between devices, shards(): lax.all_to_all(jnp.take(precond, owned_for_send, axis=0), 'grid', split_a...  27.1 us
    all_to_all x1, starting transfers between devices, shards(): lax.all_to_all(sent_rows, 'grid', split_axis=0, concat_axis=0, tiled=True)  26.4 us
    convert_element_type x1, local copies, waits for them, and re-layouts, invert_blocks(): matrix = blocks.astype(jnp.float32)  25.7 us
    all_gather x1, blocking collectives, shards(): lax.all_gather(face_terms, 'elem', axis=0, tiled=True)  13.2 us
  transfers between devices with their start and end apart: 3, of which 2 were waited for; matrix products, arithmetic and copies ran while one was open for 1% of the time, Pallas kernels for 0%

commit v1 on v0

v1 whole, which is shorter than its diff:
```python
import functools

import jax
import jax.numpy as jnp
from jax import lax
from jax.experimental import pallas as pl
from jax.experimental.pallas import tpu as pltpu
from jax.sharding import PartitionSpec as P

F32 = jnp.float32
BF16 = jnp.bfloat16
MESH = pl.DeviceIdType.MESH
VARS = 5
SLOTS = 32
OWN = 16
GRIDS = 32
ELEMS = 4
B = 320
PTS = 64
RPTS = 128
WIRE = 800
SELF = 30
LANES = 384
NODE_PLACES = (-1.0, -0.5, 0.5, 1.0)


def offsets(i):
    step = (i // 8 + 1) % 4
    dc = 1 - (i // 4) % 2
    j = i % 4
    dy = (1 + 2 * j - j // 2) % 4
    dz = (step + 4 - dy) % 4
    return dy, dz, dc


def partner(i, grid):
    dy, dz, dc = offsets(i)
    c, z, y = grid % 2, (grid // 2) % 4, grid // 8
    return ((y + dy) % 4) * 8 + ((z + dz) % 4) * 2 + (c + dc) % 2


def sender(i, grid):
    dy, dz, dc = offsets(i)
    c, z, y = grid % 2, (grid // 2) % 4, grid // 8
    return ((y + 4 - dy) % 4) * 8 + ((z + 4 - dz) % 4) * 2 + (c + 2 - dc) % 2


def iota(shape, dim):
    return lax.broadcasted_iota(jnp.int32, shape, dim)


def dot(a, b):
    return jnp.dot(a, b, preferred_element_type=F32)


def dot_t(a, b):
    return lax.dot_general(a, b, (((1,), (1,)), ((), ())), preferred_element_type=F32)


def column(row):
    n = row.shape[1]
    same = iota((n, n), 0) == iota((n, n), 1)
    return jnp.sum(jnp.where(same, row.astype(F32), 0.0), axis=1, keepdims=True)


def one_hot(col, n):
    lanes = iota((col.shape[0], n), 1).astype(F32)
    return jnp.where(col == lanes, 1.0, 0.0)


def two_term_dot(a, b):
    high = b.astype(BF16)
    low = (b - high.astype(F32)).astype(BF16)
    return dot(a, high) + dot(a, low)


def two_term_left(a, b):
    high = a.astype(BF16)
    low = (a - high.astype(F32)).astype(BF16)
    return dot(high, b) + dot(low, b)


def invert(matrix, eye):
    full = matrix.astype(F32)
    diag = full * eye
    by_row = 1.0 / jnp.sum(diag, axis=1, keepdims=True)
    by_col = 1.0 / jnp.sum(diag, axis=0, keepdims=True)
    approx = (eye * (2.0 * by_row) - full * by_row * by_col).astype(BF16)
    for last in (False, True):
        defect = (eye - dot(matrix, approx)).astype(BF16)
        approx = (approx.astype(F32) + dot(approx, defect)).astype(BF16)
    return approx


def lagrange(position):
    terms = []
    for k in range(4):
        value = None
        for m in range(4):
            if m != k:
                factor = (position - NODE_PLACES[m]) * (1.0 / (NODE_PLACES[k] - NODE_PLACES[m]))
                value = factor if value is None else value * factor
        terms.append(value)
    return terms


def pick(which, terms):
    return jnp.where(
        which == 0, terms[0], jnp.where(which == 1, terms[1], jnp.where(which == 2, terms[2], terms[3]))
    )


def main_kernel(
    slot_of,
    jac_hbm,
    fc_hbm,
    res_ref,
    om_ref,
    nb_ref,
    don_ref,
    rec_ref,
    xyz_ref,
    arrived,
    upd_ref,
    jac,
    inv,
    wire,
    fc,
    eye_ref,
    rhs_ref,
    row_ref,
    guess_all,
    don2,
    don_send,
    don_recv,
    faces,
    jac_sem,
    fc_sem,
    own_sem,
    send_sem,
    recv_sem,
    gs_sem,
    gr_sem,
    ds_sem,
    dr_sem,
):
    grid = lax.axis_index("grid")
    elem = lax.axis_index("elem")
    jac_copy = pltpu.make_async_copy(jac_hbm, jac, jac_sem)
    jac_copy.start()
    fc_copy = pltpu.make_async_copy(fc_hbm, fc, fc_sem)
    fc_copy.start()

    barrier = pltpu.get_barrier_semaphore()
    for i in range(GRIDS):
        if i != SELF:
            pl.semaphore_signal(
                barrier, inc=1, device_id={"grid": partner(i, grid)}, device_id_type=MESH
            )
    for k in range(1, ELEMS):
        pl.semaphore_signal(
            barrier, inc=1, device_id={"elem": (elem + k) % ELEMS}, device_id_type=MESH
        )

    def block_copy(i):
        return pltpu.make_async_remote_copy(
            src_ref=wire.at[i],
            dst_ref=arrived.at[grid],
            send_sem=send_sem.at[i],
            recv_sem=recv_sem.at[i],
            device_id={"grid": partner(i, grid)},
            device_id_type=MESH,
        )

    def block_arrival(i):
        return pltpu.make_async_remote_copy(
            src_ref=wire.at[i],
            dst_ref=arrived.at[sender(i, grid)],
            send_sem=send_sem.at[i],
            recv_sem=recv_sem.at[i],
            device_id={"grid": partner(i, grid)},
            device_id_type=MESH,
        )

    def guess_copy(k, place):
        return pltpu.make_async_remote_copy(
            src_ref=guess_all.at[elem],
            dst_ref=guess_all.at[place],
            send_sem=gs_sem.at[k],
            recv_sem=gr_sem.at[k],
            device_id={"elem": (elem + k) % ELEMS},
            device_id_type=MESH,
        )

    def donor_copy(i, place):
        return pltpu.make_async_remote_copy(
            src_ref=don_send.at[pl.ds(2 * partner(i, grid), 2)],
            dst_ref=don_recv.at[pl.ds(2 * place, 2)],
            send_sem=ds_sem.at[i],
            recv_sem=dr_sem.at[i],
            device_id={"grid": partner(i, grid)},
            device_id_type=MESH,
        )

    eye_ref[...] = jnp.where(iota((B, B), 0) == iota((B, B), 1), 1.0, 0.0)

    def partner_vector(shape, dim):
        i = iota(shape, dim)
        j = i & 3
        dy = (1 + 2 * j - (j >> 1)) & 3
        dz = ((i >> 3) + 5 - dy) & 3
        dc = 1 - ((i >> 2) & 1)
        c, z, y = grid % 2, (grid // 2) % 4, grid // 8
        return (((y + dy) & 3) * 8 + ((z + dz) & 3) * 2 + ((c + dc) & 1)).astype(F32)

    owner_row = om_ref[...].astype(F32)
    owner_col = column(om_ref[...])
    to_order = jnp.where(owner_row == partner_vector((GRIDS, SLOTS), 0), 1.0, 0.0)
    to_slot = jnp.where(owner_col == partner_vector((SLOTS, GRIDS), 1), 1.0, 0.0)
    live = jnp.sum(to_order, axis=1, keepdims=True) > 0.0
    rhs_ref[...] = dot(to_order.astype(BF16), res_ref[...])

    jac_copy.wait()

    def build(i):
        matrix = jac[slot_of[i]]
        result = invert(matrix, eye_ref[...])
        inv[i] = result
        wire[i, 0:320, :] = result[:, 0:128]
        wire[i, 320:640, :] = result[:, 128:256]
        wire[i, 640:800, :] = jnp.concatenate([result[0:160, 256:320], result[160:320, 256:320]], axis=1)
        vector = rhs_ref[pl.ds(i, 1), :].astype(BF16)
        row_ref[pl.ds(i, 1), :] = dot_t(vector, result)

    build(0)
    build(1)
    pl.semaphore_wait(barrier, GRIDS - 1 + ELEMS - 1)

    def build_step(t, carry):
        build(2 * t)
        build(2 * t + 1)

        @pl.when(t < 5)
        def _():
            block_copy(t - 1).start()

        @pl.when(jnp.logical_and(t >= 5, t % 3 != 0))
        def _():
            block_copy((t - 5) - (t - 3) // 3 + 4).start()

        return carry

    lax.fori_loop(1, 16, build_step, 0)

    guess = dot(to_slot.astype(BF16), jnp.where(live, row_ref[...], 0.0).astype(BF16)).astype(BF16)
    guess_all[elem] = guess
    donor_rows = one_hot(column(don_ref[...]), SLOTS).astype(BF16)
    don2[:, 0:B] = dot(donor_rows, guess)

    def spread(r, carry):
        don_send[r] = don2[pl.ds(r, 1), :]
        return carry

    lax.fori_loop(0, 2 * GRIDS, spread, 0, unroll=8)
    for k in range(1, ELEMS):
        guess_copy(k, elem).start()

    def start_donors(i, carry):
        @pl.when(i != SELF)
        def _():
            donor_copy(i, grid).start()

        return carry

    lax.fori_loop(0, GRIDS, start_donors, 0)

    def start_blocks(i, carry):
        @pl.when(i != SELF)
        def _():
            block_copy(i).start()

        return carry

    lax.fori_loop(11, GRIDS, start_blocks, 0)
    own_copy = pltpu.make_async_copy(wire.at[SELF], arrived.at[grid], own_sem)
    own_copy.start()

    lane = iota((RPTS, B), 1)
    point = lane & (PTS - 1)
    xs = lagrange(column(xyz_ref[0:1, :]))
    ys = lagrange(column(xyz_ref[1:2, :]))
    zs = lagrange(column(xyz_ref[2:3, :]))
    basis = pick(point >> 4, xs) * pick((point >> 2) & 3, ys) * pick(point & 3, zs)
    at_point = point.astype(F32) == column(rec_ref[2:3, :])
    donor_pick = one_hot(column(rec_ref[0:1, :]), 2 * GRIDS).astype(BF16)
    target = jnp.where(
        rec_ref[1:2, :].astype(F32) == iota((SLOTS, RPTS), 0).astype(F32), 1.0, 0.0
    ).astype(BF16)
    same_var = jnp.where((iota((B, B), 0) >> 6) == (iota((B, B), 1) >> 6), 1.0, 0.0).astype(BF16)
    face_pick = jnp.concatenate(
        [one_hot(column(nb_ref[f : f + 1, :]), ELEMS * SLOTS) for f in range(6)], axis=0
    ).astype(BF16)

    fc_copy.wait()
    for k in range(1, ELEMS):
        guess_copy(k, (elem + ELEMS - k) % ELEMS).wait()
    rows = dot(face_pick, guess_all[...].reshape(ELEMS * SLOTS, B)).astype(BF16)
    faces[...] = dot(rows, fc[...])
    face_sum = jnp.zeros((SLOTS, B), F32)
    for f in range(6):
        opposite = f ^ 1
        part = faces[f * SLOTS : (f + 1) * SLOTS, opposite * B : (opposite + 1) * B]
        face_sum = face_sum + part.astype(BF16).astype(F32)

    def wait_donors(i, carry):
        @pl.when(i != SELF)
        def _():
            donor_copy(i, sender(i, grid)).wait()

        return carry

    lax.fori_loop(0, GRIDS, wait_donors, 0)

    def collect(r, carry):
        don2[pl.ds(r, 1), :] = don_recv[r]
        return carry

    lax.fori_loop(0, 2 * GRIDS, collect, 0, unroll=8)
    mine = (iota((2 * GRIDS, B), 0) >> 1) == grid
    donor_values = jnp.where(mine, 0.0, don2[:, 0:B]).astype(BF16)
    picked = dot(donor_pick, donor_values)
    values = two_term_left(picked * basis, same_var)
    fringe = two_term_dot(target, jnp.where(at_point, values, 0.0))
    sweep = (res_ref[...].astype(F32) - face_sum + fringe).astype(BF16)
    rhs_ref[...] = dot(to_order.astype(BF16), sweep)

    def apply(i, carry):
        vector = rhs_ref[pl.ds(i, 1), :].astype(BF16)
        row_ref[pl.ds(i, 1), :] = dot_t(vector, inv[i])
        return carry

    lax.fori_loop(0, GRIDS, apply, 0, unroll=4)
    upd_ref[...] = jnp.dot(
        to_slot,
        jnp.where(live, row_ref[...], 0.0),
        precision=lax.Precision.HIGHEST,
        preferred_element_type=F32,
    )

    own_copy.wait()

    def finish(i, carry):
        @pl.when(i != SELF)
        def _():
            block_arrival(i).wait()

        return carry

    lax.fori_loop(0, GRIDS, finish, 0)


def place_kernel(owned, upd_ref, w0, w1, w2, w3, out_ref, upd_out):
    for k, w in enumerate((w0, w1, w2, w3)):
        out_ref[k, :, 0:128] = w[0, 0:320, :]
        out_ref[k, :, 128:256] = w[0, 320:640, :]
        out_ref[k, 0:160, 256:320] = w[0, 640:800, 0:64]
        out_ref[k, 160:320, 256:320] = w[0, 640:800, 64:128]

    @pl.when(pl.program_id(0) == 0)
    def _():
        upd_out[...] = upd_ref[...]


def shards(jacobians, residual, owner_map, owner_slot, face_coupling, neighbours, donors, receptors, coords):
    grid = lax.axis_index("grid")
    order = partner(jnp.arange(GRIDS, dtype=jnp.int32), grid)
    hits = owner_map[None, :] == order[:, None]
    slot_of = jnp.sum(jnp.where(hits, jnp.arange(SLOTS, dtype=jnp.int32)[None, :], 0), axis=1)

    vmem = pl.BlockSpec(memory_space=pltpu.VMEM)
    anywhere = pl.BlockSpec(memory_space=pl.ANY)
    arrived, update = pl.pallas_call(
        main_kernel,
        out_shape=(
            jax.ShapeDtypeStruct((GRIDS, WIRE, 128), BF16),
            jax.ShapeDtypeStruct((SLOTS, B), F32),
        ),
        in_specs=[pl.BlockSpec(memory_space=pltpu.SMEM), anywhere, anywhere] + [vmem] * 6,
        out_specs=(anywhere, vmem),
        scratch_shapes=[
            pltpu.VMEM((SLOTS, B, B), BF16),
            pltpu.VMEM((GRIDS, B, B), BF16),
            pltpu.VMEM((GRIDS, WIRE, 128), BF16),
            pltpu.VMEM((B, 6 * B), BF16),
            pltpu.VMEM((B, B), F32),
            pltpu.VMEM((GRIDS, B), F32),
            pltpu.VMEM((GRIDS, B), F32),
            pltpu.VMEM((ELEMS, SLOTS, B), BF16),
            pltpu.VMEM((2 * GRIDS, LANES), F32),
            pltpu.VMEM((2 * GRIDS, 1, LANES), F32),
            pltpu.VMEM((2 * GRIDS, 1, LANES), F32),
            pltpu.VMEM((6 * SLOTS, 6 * B), F32),
            pltpu.SemaphoreType.DMA,
            pltpu.SemaphoreType.DMA,
            pltpu.SemaphoreType.DMA,
            pltpu.SemaphoreType.DMA((GRIDS,)),
            pltpu.SemaphoreType.DMA((GRIDS,)),
            pltpu.SemaphoreType.DMA((ELEMS,)),
            pltpu.SemaphoreType.DMA((ELEMS,)),
            pltpu.SemaphoreType.DMA((GRIDS,)),
            pltpu.SemaphoreType.DMA((GRIDS,)),
        ],
        compiler_params=pltpu.CompilerParams(
            collective_id=0, has_side_effects=True, vmem_limit_bytes=60 * 2**20
        ),
        name="invert_send_sweep",
    )(
        slot_of,
        jacobians,
        face_coupling,
        residual,
        owner_map.reshape(1, SLOTS),
        neighbours,
        donors.reshape(1, 2 * GRIDS),
        receptors,
        coords,
    )

    def block(k):
        return pl.BlockSpec((1, WIRE, 128), lambda o, owned: (owned[4 * o + k], 0, 0))

    return pl.pallas_call(
        place_kernel,
        out_shape=(
            jax.ShapeDtypeStruct((OWN, B, B), BF16),
            jax.ShapeDtypeStruct((SLOTS, B), F32),
        ),
        grid_spec=pltpu.PrefetchScalarGridSpec(
            num_scalar_prefetch=1,
            grid=(OWN // 4,),
            in_specs=[pl.BlockSpec((SLOTS, B), lambda o, owned: (0, 0))] + [block(k) for k in range(4)],
            out_specs=(
                pl.BlockSpec((4, B, B), lambda o, owned: (o, 0, 0)),
                pl.BlockSpec((SLOTS, B), lambda o, owned: (0, 0)),
            ),
        ),
        name="place_owned",
    )(owner_slot, update, arrived, arrived, arrived, arrived)


def solution(mesh):
    in_specs = (
        P(("grid", "elem"), None, None),
        P(("grid", "elem"), None),
        P(("grid", "elem")),
        P(("grid", "elem")),
        P(),
        P(None, ("grid", "elem")),
        P(("grid", "elem")),
        P(None, ("grid", "elem")),
        P(None, ("grid", "elem")),
    )
    out_specs = (P(("grid", "elem"), None, None), P(("grid", "elem"), None))
    return jax.shard_map(shards, mesh=mesh, in_specs=in_specs, out_specs=out_specs, check_vma=False)
```

time: 483 us -> 118 us (0.24)
  the two profiles are of different devices: /device:TPU:10 before, /device:TPU:1 now
where the time goes in v1:
time: 118 us
  Pallas kernels  115 us (97%)
  other arithmetic  1.38 us (1%)
    pallas_call x1, Pallas kernels, shards(): pl.pallas_call(main_kernel, out_shape=(jax.ShapeDtypeStruct((GRIDS, WIRE,...  110 us
    pallas_call x1, Pallas kernels, shards(): pl.pallas_call(place_kernel, out_shape=(jax.ShapeDtypeStruct((OWN, B, B),...  5.78 us

profile of v1, /device:TPU:1, one launch (start us, length us, event | category | flops | bytes accessed | tf_op | source)
XLA Modules:
  0.0 117.5 jit_solution(5705274510154883096)
XLA Ops:
  0.7 1.3 %select_reduce_fusion.slot_of = s32[32]{0:T(128)} fusion(s32[32]{0:T(128)} %param.11, s32[32]{0:T(128)S(1)} %fusion), kind=kLoop, calls=%fused_computation | loop fusion | flops 3040 | bytes 384 | tf_op jit(solution)/shard_map/reduce_sum | solution.py:378
  2.1 109.7 %invert_send_sweep.1 = (bf16[32,800,128]{2,1,0:T(8,128)(2,1)}, f32[32,320]{1,0:T(8,128)}) custom-call(s32[32]{0:T(128)} %select_reduce_fusion.slot_of, bf16[32,320,320]{2,1,0:T(8,128)(2,1)} %jac_hbm.1, bf16[320,1920]{1,0:T(8,128)(2,1)} %fc_hbm.1, bf16[32,320]{1,0:T(8,128)(2,1)} %res_ref.1, s32[1,32]{1,0:T(1,128)} %bitcast.2, s32[6,32]{1,0:T(8,128)} %nb_ref.1, ...), custom_call_target="tpu_custom_call" | custom-call | tf_op jit(solution)/shard_map/invert_send_sweep/pallas_call | solution.py:382
  111.8 5.8 %place_owned.1 = (bf16[16,320,320]{2,1,0:T(8,128)(2,1)}, f32[32,320]{1,0:T(8,128)}) custom-call(s32[16]{0:T(128)} %owned.1, f32[32,320]{1,0:T(8,128)} %get-tuple-element.4.upd_ref, bf16[32,800,128]{2,1,0:T(8,128)(2,1)} %get-tuple-element.5.w0.w1.w2.w3, bf16[32,800,128]{2,1,0:T(8,128)(2,1)} %get-tuple-element.5.w0.w1.w2.w3, ...), custom_call_target="tpu_custom_call" | custom-call | tf_op jit(solution)/shard_map/place_owned/pallas_call | solution.py:432
  (1 shorter events, 0.0 us)

commit v2 on v1

v2 whole, which is shorter than its diff:
```python
import functools

import jax
import jax.numpy as jnp
from jax import lax
from jax.experimental import pallas as pl
from jax.experimental.pallas import tpu as pltpu
from jax.sharding import PartitionSpec as P

F32 = jnp.float32
BF16 = jnp.bfloat16
MESH = pl.DeviceIdType.MESH
VARS = 5
SLOTS = 32
OWN = 16
GRIDS = 32
ELEMS = 4
B = 320
PTS = 64
RPTS = 128
HEAD = 640
TAIL = 160
WIRE = HEAD + TAIL
PACK = 16
SELF = 2
GROUP = 4
TOGETHER = 4
EARLY = 4
FIRST = 2
LANES = 384
NODE_PLACES = (-1.0, -0.5, 0.5, 1.0)


def offsets(i):
    step = i // 8
    dc = (i // 4) % 2
    j = i % 4
    dy = (1 + 2 * j - j // 2) % 4
    dz = (step + 4 - dy) % 4
    return dy, dz, dc


def partner(i, grid):
    dy, dz, dc = offsets(i)
    c, z, y = grid % 2, (grid // 2) % 4, grid // 8
    return ((y + dy) % 4) * 8 + ((z + dz) % 4) * 2 + (c + dc) % 2


def sender(i, grid):
    dy, dz, dc = offsets(i)
    c, z, y = grid % 2, (grid // 2) % 4, grid // 8
    return ((y + 4 - dy) % 4) * 8 + ((z + 4 - dz) % 4) * 2 + (c + 2 - dc) % 2


def iota(shape, dim):
    return lax.broadcasted_iota(jnp.int32, shape, dim)


def dot(a, b):
    return jnp.dot(a, b, preferred_element_type=F32)


def dot_t(a, b):
    return lax.dot_general(a, b, (((1,), (1,)), ((), ())), preferred_element_type=F32)


def column(row):
    n = row.shape[1]
    same = iota((n, n), 0) == iota((n, n), 1)
    return jnp.sum(jnp.where(same, row.astype(F32), 0.0), axis=1, keepdims=True)


def one_hot(col, n):
    lanes = iota((col.shape[0], n), 1).astype(F32)
    return jnp.where(col == lanes, 1.0, 0.0)


def two_term_dot(a, b):
    high = b.astype(BF16)
    low = (b - high.astype(F32)).astype(BF16)
    return dot(a, high) + dot(a, low)


def two_term_left(a, b):
    high = a.astype(BF16)
    low = (a - high.astype(F32)).astype(BF16)
    return dot(high, b) + dot(low, b)


def scaled_start(matrix, eye):
    full = matrix.astype(F32)
    diag = full * eye
    by_row = 1.0 / jnp.sum(diag, axis=1, keepdims=True)
    by_col = 1.0 / jnp.sum(diag, axis=0, keepdims=True)
    return (eye * (2.0 * by_row) - full * by_row * by_col).astype(BF16)


def invert(matrices, eye):
    approx = [scaled_start(m, eye) for m in matrices]
    for step in range(2):
        defect = [(eye - dot(m, x)).astype(BF16) for m, x in zip(matrices, approx)]
        approx = [(x.astype(F32) + dot(x, d)).astype(BF16) for x, d in zip(approx, defect)]
    return approx


def lagrange(position):
    terms = []
    for k in range(4):
        value = None
        for m in range(4):
            if m != k:
                factor = (position - NODE_PLACES[m]) * (1.0 / (NODE_PLACES[k] - NODE_PLACES[m]))
                value = factor if value is None else value * factor
        terms.append(value)
    return terms


def pick(which, terms):
    return jnp.where(
        which == 0, terms[0], jnp.where(which == 1, terms[1], jnp.where(which == 2, terms[2], terms[3]))
    )


def main_kernel(
    jac_hbm,
    fc_hbm,
    om1_hbm,
    res_hbm,
    om_hbm,
    nb_hbm,
    don_hbm,
    rec_hbm,
    xyz_hbm,
    arrived,
    upd_hbm,
    owner_map,
    res_ref,
    om_ref,
    nb_ref,
    don_ref,
    rec_ref,
    xyz_ref,
    upd_ref,
    jac,
    inv,
    wire,
    fc,
    eye_ref,
    rhs_ref,
    acc_ref,
    guess_all,
    tails,
    faces,
    jac_sem,
    fc_sem,
    in_sem,
    upd_sem,
    own_sem,
    tails_sem,
    hs_sem,
    hr_sem,
    gs_sem,
    gr_sem,
    ts_sem,
    tr_sem,
):
    grid = lax.axis_index("grid")
    elem = lax.axis_index("elem")
    barrier = pltpu.get_barrier_semaphore()
    for i in range(GRIDS):
        if i != SELF:
            pl.semaphore_signal(
                barrier, inc=1, device_id={"grid": partner(i, grid)}, device_id_type=MESH
            )
    for k in range(1, ELEMS):
        pl.semaphore_signal(
            barrier, inc=1, device_id={"elem": (elem + k) % ELEMS}, device_id_type=MESH
        )

    small = ((om1_hbm, owner_map), (om_hbm, om_ref), (res_hbm, res_ref), (nb_hbm, nb_ref))
    small += ((don_hbm, don_ref), (rec_hbm, rec_ref), (xyz_hbm, xyz_ref))
    small_copies = [pltpu.make_async_copy(a, b, in_sem.at[k]) for k, (a, b) in enumerate(small)]
    for copy in small_copies:
        copy.start()
    jac_copy = pltpu.make_async_copy(jac_hbm, jac, jac_sem)
    jac_copy.start()
    fc_copy = pltpu.make_async_copy(fc_hbm, fc, fc_sem)
    fc_copy.start()

    def head_copy(i, place):
        return pltpu.make_async_remote_copy(
            src_ref=wire.at[i, pl.ds(0, HEAD)],
            dst_ref=arrived.at[place, pl.ds(0, HEAD)],
            send_sem=hs_sem.at[i],
            recv_sem=hr_sem.at[i],
            device_id={"grid": partner(i, grid)},
            device_id_type=MESH,
        )

    def tail_copy(i, place):
        return pltpu.make_async_remote_copy(
            src_ref=wire.at[i, pl.ds(HEAD, TAIL + PACK)],
            dst_ref=tails.at[place],
            send_sem=ts_sem.at[i],
            recv_sem=tr_sem.at[i],
            device_id={"grid": partner(i, grid)},
            device_id_type=MESH,
        )

    def guess_copy(k, place):
        return pltpu.make_async_remote_copy(
            src_ref=guess_all.at[elem],
            dst_ref=guess_all.at[place],
            send_sem=gs_sem.at[k],
            recv_sem=gr_sem.at[k],
            device_id={"elem": (elem + k) % ELEMS},
            device_id_type=MESH,
        )

    eye_ref[...] = jnp.where(iota((B, B), 0) == iota((B, B), 1), 1.0, 0.0)

    def partner_vector(i):
        j = i & 3
        dy = (1 + 2 * j - (j >> 1)) & 3
        dz = ((i >> 3) + 4 - dy) & 3
        dc = (i >> 2) & 1
        c, z, y = grid % 2, (grid // 2) % 4, grid // 8
        return (((y + dy) & 3) * 8 + ((z + dz) & 3) * 2 + ((c + dc) & 1)).astype(F32)

    for copy in small_copies:
        copy.wait()
    owner_row = om_ref[...].astype(F32)
    owner_col = column(om_ref[...])
    to_order = jnp.where(
        jnp.logical_and(owner_row == partner_vector(iota((128, SLOTS), 0)), iota((128, SLOTS), 0) < GRIDS), 1.0, 0.0
    )
    to_slot = jnp.where(
        jnp.logical_and(owner_col == partner_vector(iota((SLOTS, 128), 1)), iota((SLOTS, 128), 1) < GRIDS), 1.0, 0.0
    )
    live = jnp.sum(to_slot, axis=0, keepdims=True) > 0.0

    pack_row = iota((GRIDS * PACK, 2 * GRIDS), 0)
    pack_slot = pack_row & (PACK - 1)
    pack_kind = jnp.where(pack_slot >= 3, 1.0, 0.0)
    wanted_entry = 2.0 * partner_vector(pack_row >> 4) + pack_kind
    entry_lane = iota((GRIDS * PACK, 2 * GRIDS), 1).astype(F32)
    entries = jnp.where(wanted_entry == entry_lane, don_ref[...].astype(F32), 0.0)
    entry = jnp.sum(entries, axis=1, keepdims=True)
    used = (iota((GRIDS * PACK, SLOTS), 0) & (PACK - 1)) < 6
    donor_rows = jnp.where(used, one_hot(entry, SLOTS), 0.0).astype(BF16)

    def ordered_columns(rows):
        ordered = dot(to_order.astype(BF16), rows).astype(BF16)
        return dot_t(eye_ref[...].astype(BF16), ordered).astype(BF16)

    rhs_ref[...] = ordered_columns(res_ref[...])
    acc_ref[...] = jnp.zeros((B, 128), F32)

    jac_copy.wait()

    def slot_of(i):
        wanted = partner(i, grid)
        slot = jnp.int32(0)
        for k in range(SLOTS):
            slot = jnp.where(owner_map[k] == wanted, jnp.int32(k), slot)
        return slot

    order_lane = iota((B, 128), 1)

    def build(first, count):
        places = [first + k for k in range(count)]
        results = invert([jac[slot_of(i)] for i in places], eye_ref[...])
        for i, result in zip(places, results):
            inv[i] = result
            wire[i, 0:320, :] = result[:, 0:128]
            wire[i, 320:640, :] = result[:, 128:256]
            wire[i, HEAD:WIRE, :] = jnp.concatenate([result[0:160, 256:320], result[160:320, 256:320]], axis=1)
        products = [dot(result, rhs_ref[...]) for result in results]
        total = acc_ref[...]
        for i, product in zip(places, products):
            total = jnp.where(order_lane == i, product, total)
        acc_ref[...] = total

    def build_group(q):
        for k in range(0, GROUP, TOGETHER):
            build(GROUP * q + k, TOGETHER)

    def send_group(q):
        for k in range(GROUP):
            if isinstance(q, int) and GROUP * q + k == SELF:
                continue
            head_copy(GROUP * q + k, grid).start()

    def build_first(q, carry):
        build_group(q)
        return carry

    lax.fori_loop(0, 2, build_first, 0)
    pl.semaphore_wait(barrier, GRIDS - 1 + ELEMS - 1)
    for q in range(FIRST):
        send_group(q)

    def build_next(q, carry):
        build_group(q)

        @pl.when(jnp.logical_and(q % 2 == 0, q >= 4))
        def _():
            send_group(q // 2)

        return carry

    lax.fori_loop(2, GRIDS // GROUP, build_next, 0)

    guess = dot_t(to_slot.astype(BF16), jnp.where(live, acc_ref[...], 0.0).astype(BF16)).astype(BF16)
    guess_all[elem] = guess
    for k in range(1, ELEMS):
        guess_copy(k, elem).start()
    wide = jnp.concatenate([guess, jnp.zeros((SLOTS, LANES - B), BF16)], axis=1)
    spread = dot(donor_rows, wide)
    row = iota((GRIDS * PACK, 128), 0) & (PACK - 1)
    third = jnp.where(row >= 3, row - 3, row)
    packed = jnp.where(
        third == 0, spread[:, 0:128], jnp.where(third == 1, spread[:, 128:256], spread[:, 256:384])
    )
    wire[:, WIRE : WIRE + PACK, :] = packed.astype(BF16).reshape(GRIDS, PACK, 128)
    tails[grid] = wire[SELF, HEAD : WIRE + PACK, :]

    def send_tails(i, carry):
        @pl.when(i != SELF)
        def _():
            tail_copy(i, grid).start()

        return carry

    lax.fori_loop(0, GRIDS, send_tails, 0)

    def send_rest(q, carry):
        send_group(q)
        return carry

    lax.fori_loop(EARLY, GRIDS // GROUP, send_rest, 0)
    own_copy = pltpu.make_async_copy(wire.at[SELF, pl.ds(0, HEAD)], arrived.at[grid, pl.ds(0, HEAD)], own_sem)
    own_copy.start()

    lane = iota((RPTS, B), 1)
    point = lane & (PTS - 1)
    xs = lagrange(column(xyz_ref[0:1, :]))
    ys = lagrange(column(xyz_ref[1:2, :]))
    zs = lagrange(column(xyz_ref[2:3, :]))
    basis = pick(point >> 4, xs) * pick((point >> 2) & 3, ys) * pick(point & 3, zs)
    at_point = point.astype(F32) == column(rec_ref[2:3, :])
    donor_col = column(rec_ref[0:1, :])
    donor_grid = jnp.floor(donor_col * 0.5)
    donor_base = PACK * donor_grid + 3.0 * (donor_col - 2.0 * donor_grid)
    target = jnp.where(
        rec_ref[1:2, :].astype(F32) == iota((SLOTS, RPTS), 0).astype(F32), 1.0, 0.0
    ).astype(BF16)
    same_var = jnp.where((iota((B, B), 0) >> 6) == (iota((B, B), 1) >> 6), 1.0, 0.0).astype(BF16)
    face_pick = jnp.concatenate(
        [one_hot(column(nb_ref[f : f + 1, :]), ELEMS * SLOTS) for f in range(6)], axis=0
    ).astype(BF16)

    fc_copy.wait()
    for k in range(1, ELEMS):
        guess_copy(k, (elem + ELEMS - k) % ELEMS).wait()
    rows = dot(face_pick, guess_all[...].reshape(ELEMS * SLOTS, B)).astype(BF16)
    faces[...] = dot(rows, fc[...])
    face_sum = jnp.zeros((SLOTS, B), F32)
    for f in range(6):
        opposite = f ^ 1
        part = faces[f * SLOTS : (f + 1) * SLOTS, opposite * B : (opposite + 1) * B]
        face_sum = face_sum + part.astype(BF16).astype(F32)

    def wait_tails(i, carry):
        @pl.when(i != SELF)
        def _():
            tail_copy(i, sender(i, grid)).wait()

        return carry

    lax.fori_loop(0, GRIDS, wait_tails, 0)
    tails_copy = pltpu.make_async_copy(
        tails.at[:, pl.ds(0, TAIL)], arrived.at[:, pl.ds(HEAD, TAIL)], tails_sem
    )
    tails_copy.start()
    packs = tails[:, TAIL : TAIL + PACK, :].reshape(GRIDS * PACK, 128)
    picked = jnp.concatenate(
        [dot(one_hot(donor_base + float(q), GRIDS * PACK).astype(BF16), packs) for q in range(3)], axis=1
    )[:, 0:B]
    values = two_term_left(picked * basis, same_var)
    fringe = two_term_dot(target, jnp.where(at_point, values, 0.0))
    sweep = (res_ref[...].astype(F32) - face_sum + fringe).astype(BF16)
    rhs_ref[...] = ordered_columns(sweep)

    def apply(q, carry):
        places = [GROUP * q + k for k in range(GROUP)]
        products = [dot(inv[i], rhs_ref[...]) for i in places]
        total = acc_ref[...]
        for i, product in zip(places, products):
            total = jnp.where(order_lane == i, product, total)
        acc_ref[...] = total
        return carry

    lax.fori_loop(0, GRIDS // GROUP, apply, 0)
    upd_ref[...] = lax.dot_general(
        to_slot,
        jnp.where(live, acc_ref[...], 0.0),
        (((1,), (1,)), ((), ())),
        precision=lax.Precision.HIGHEST,
        preferred_element_type=F32,
    )
    upd_copy = pltpu.make_async_copy(upd_ref, upd_hbm, upd_sem)
    upd_copy.start()
    own_copy.wait()
    upd_copy.wait()

    tails_copy.wait()

    def finish(i, carry):
        @pl.when(i != SELF)
        def _():
            head_copy(i, sender(i, grid)).wait()

        return carry

    lax.fori_loop(0, GRIDS, finish, 0)


def place_kernel(owned, upd_ref, w0, w1, w2, w3, out_ref, upd_out):
    for k, w in enumerate((w0, w1, w2, w3)):
        out_ref[k, :, 0:128] = w[0, 0:320, :]
        out_ref[k, :, 128:256] = w[0, 320:640, :]
        out_ref[k, 0:160, 256:320] = w[0, 640:800, 0:64]
        out_ref[k, 160:320, 256:320] = w[0, 640:800, 64:128]

    @pl.when(pl.program_id(0) == 0)
    def _():
        upd_out[...] = upd_ref[...]


def shards(jacobians, residual, owner_map, owner_slot, face_coupling, neighbours, donors, receptors, coords):
    anywhere = pl.BlockSpec(memory_space=pl.ANY)
    arrived, update = pl.pallas_call(
        main_kernel,
        out_shape=(
            jax.ShapeDtypeStruct((GRIDS, WIRE, 128), BF16),
            jax.ShapeDtypeStruct((SLOTS, B), F32),
        ),
        in_specs=[anywhere] * 9,
        out_specs=(anywhere, anywhere),
        scratch_shapes=[
            pltpu.SMEM((SLOTS,), jnp.int32),
            pltpu.VMEM((SLOTS, B), BF16),
            pltpu.VMEM((1, SLOTS), jnp.int32),
            pltpu.VMEM((6, SLOTS), jnp.int32),
            pltpu.VMEM((1, 2 * GRIDS), jnp.int32),
            pltpu.VMEM((3, RPTS), jnp.int32),
            pltpu.VMEM((3, RPTS), F32),
            pltpu.VMEM((SLOTS, B), F32),
            pltpu.VMEM((SLOTS, B, B), BF16),
            pltpu.VMEM((GRIDS, B, B), BF16),
            pltpu.VMEM((GRIDS, WIRE + PACK, 128), BF16),
            pltpu.VMEM((B, 6 * B), BF16),
            pltpu.VMEM((B, B), F32),
            pltpu.VMEM((B, 128), BF16),
            pltpu.VMEM((B, 128), F32),
            pltpu.VMEM((ELEMS, SLOTS, B), BF16),
            pltpu.VMEM((GRIDS, TAIL + PACK, 128), BF16),
            pltpu.VMEM((6 * SLOTS, 6 * B), F32),
            pltpu.SemaphoreType.DMA,
            pltpu.SemaphoreType.DMA,
            pltpu.SemaphoreType.DMA((7,)),
            pltpu.SemaphoreType.DMA,
            pltpu.SemaphoreType.DMA,
            pltpu.SemaphoreType.DMA,
            pltpu.SemaphoreType.DMA((GRIDS,)),
            pltpu.SemaphoreType.DMA((GRIDS,)),
            pltpu.SemaphoreType.DMA((ELEMS,)),
            pltpu.SemaphoreType.DMA((ELEMS,)),
            pltpu.SemaphoreType.DMA((GRIDS,)),
            pltpu.SemaphoreType.DMA((GRIDS,)),
        ],
        compiler_params=pltpu.CompilerParams(
            collective_id=0, has_side_effects=True, vmem_limit_bytes=60 * 2**20
        ),
        name="invert_send_sweep",
    )(
        jacobians,
        face_coupling,
        owner_map,
        residual,
        owner_map.reshape(1, SLOTS),
        neighbours,
        donors.reshape(1, 2 * GRIDS),
        receptors,
        coords,
    )

    def block(k):
        return pl.BlockSpec((1, WIRE, 128), lambda o, owned: (owned[4 * o + k], 0, 0))

    return pl.pallas_call(
        place_kernel,
        out_shape=(
            jax.ShapeDtypeStruct((OWN, B, B), BF16),
            jax.ShapeDtypeStruct((SLOTS, B), F32),
        ),
        grid_spec=pltpu.PrefetchScalarGridSpec(
            num_scalar_prefetch=1,
            grid=(OWN // 4,),
            in_specs=[pl.BlockSpec((SLOTS, B), lambda o, owned: (0, 0))] + [block(k) for k in range(4)],
            out_specs=(
                pl.BlockSpec((4, B, B), lambda o, owned: (o, 0, 0)),
                pl.BlockSpec((SLOTS, B), lambda o, owned: (0, 0)),
            ),
        ),
        name="place_owned",
    )(owner_slot, update, arrived, arrived, arrived, arrived)


def solution(mesh):
    in_specs = (
        P(("grid", "elem"), None, None),
        P(("grid", "elem"), None),
        P(("grid", "elem")),
        P(("grid", "elem")),
        P(),
        P(None, ("grid", "elem")),
        P(("grid", "elem")),
        P(None, ("grid", "elem")),
        P(None, ("grid", "elem")),
    )
    out_specs = (P(("grid", "elem"), None, None), P(("grid", "elem"), None))
    return jax.shard_map(shards, mesh=mesh, in_specs=in_specs, out_specs=out_specs, check_vma=False)
```

time: 118 us -> 102 us (0.86)
  Pallas kernels: 115 us -> 101 us
  other arithmetic: 1.38 us -> 0 us
    pallas_call x1, Pallas kernels: 110 us -> 95.1 us  [shards(): pl.pallas_call(main_kernel, out_shape=(jax.ShapeDtypeStruct((GRIDS, WIRE,...]
    reduce_sum x1 -> x0, other arithmetic: 1.35 us -> none  [shards(): jnp.sum(jnp.where(hits, jnp.arange(SLOTS, dtype=jnp.int32)[None, :], 0),...]
where the time goes in v2:
time: 102 us
  Pallas kernels  101 us (99%)
    pallas_call x1, Pallas kernels, shards(): pl.pallas_call(main_kernel, out_shape=(jax.ShapeDtypeStruct((GRIDS, WIRE,...  95.1 us
    pallas_call x1, Pallas kernels, shards(): pl.pallas_call(place_kernel, out_shape=(jax.ShapeDtypeStruct((OWN, B, B),...  5.78 us

profile of v2, /device:TPU:1, one launch (start us, length us, event | category | flops | bytes accessed | tf_op | source)
XLA Modules:
  0.0 101.5 jit_solution(12964032529069494952)
XLA Ops:
  0.6 95.1 %invert_send_sweep.1 = (bf16[32,800,128]{2,1,0:T(8,128)(2,1)}, f32[32,320]{1,0:T(8,128)}) custom-call(bf16[32,320,320]{2,1,0:T(8,128)(2,1)} %jac_hbm.1, bf16[320,1920]{1,0:T(8,128)(2,1)} %fc_hbm.1, s32[32]{0:T(128)} %om1_hbm.1, bf16[32,320]{1,0:T(8,128)(2,1)} %res_hbm.1, s32[1,32]{1,0:T(1,128)} %bitcast.2, s32[6,32]{1,0:T(8,128)} %nb_hbm.1, ...), custom_call_target="tpu_custom_call" | custom-call | tf_op jit(solution)/shard_map/invert_send_sweep/pallas_call | solution.py:443
  95.7 5.8 %place_owned.1 = (bf16[16,320,320]{2,1,0:T(8,128)(2,1)}, f32[32,320]{1,0:T(8,128)}) custom-call(s32[16]{0:T(128)} %owned.1, f32[32,320]{1,0:T(8,128)} %get-tuple-element.4.upd_ref, bf16[32,800,128]{2,1,0:T(8,128)(2,1)} %get-tuple-element.5.w0.w1.w2.w3, bf16[32,800,128]{2,1,0:T(8,128)(2,1)} %get-tuple-element.5.w0.w1.w2.w3, ...), custom_call_target="tpu_custom_call" | custom-call | tf_op jit(solution)/shard_map/place_owned/pallas_call | solution.py:502

commit v3 on v2

--- a/solution.py
+++ b/solution.py
@@ -22,11 +22,11 @@
 TAIL = 160
 WIRE = HEAD + TAIL
 PACK = 16
+HALVES = 2
 SELF = 2
 GROUP = 4
 TOGETHER = 4
 EARLY = 4
-FIRST = 2
 LANES = 384
 NODE_PLACES = (-1.0, -0.5, 0.5, 1.0)
 
@@ -187,12 +187,13 @@
     fc_copy = pltpu.make_async_copy(fc_hbm, fc, fc_sem)
     fc_copy.start()
 
-    def head_copy(i, place):
+    def head_copy(i, h, place):
+        rows = pl.ds(h * (HEAD // HALVES), HEAD // HALVES)
         return pltpu.make_async_remote_copy(
-            src_ref=wire.at[i, pl.ds(0, HEAD)],
-            dst_ref=arrived.at[place, pl.ds(0, HEAD)],
-            send_sem=hs_sem.at[i],
-            recv_sem=hr_sem.at[i],
+            src_ref=wire.at[i, rows],
+            dst_ref=arrived.at[place, rows],
+            send_sem=hs_sem.at[i, h],
+            recv_sem=hr_sem.at[i, h],
             device_id={"grid": partner(i, grid)},
             device_id_type=MESH,
         )
@@ -238,16 +239,6 @@
         jnp.logical_and(owner_col == partner_vector(iota((SLOTS, 128), 1)), iota((SLOTS, 128), 1) < GRIDS), 1.0, 0.0
     )
     live = jnp.sum(to_slot, axis=0, keepdims=True) > 0.0
-
-    pack_row = iota((GRIDS * PACK, 2 * GRIDS), 0)
-    pack_slot = pack_row & (PACK - 1)
-    pack_kind = jnp.where(pack_slot >= 3, 1.0, 0.0)
-    wanted_entry = 2.0 * partner_vector(pack_row >> 4) + pack_kind
-    entry_lane = iota((GRIDS * PACK, 2 * GRIDS), 1).astype(F32)
-    entries = jnp.where(wanted_entry == entry_lane, don_ref[...].astype(F32), 0.0)
-    entry = jnp.sum(entries, axis=1, keepdims=True)
-    used = (iota((GRIDS * PACK, SLOTS), 0) & (PACK - 1)) < 6
-    donor_rows = jnp.where(used, one_hot(entry, SLOTS), 0.0).astype(BF16)
 
     def ordered_columns(rows):
         ordered = dot(to_order.astype(BF16), rows).astype(BF16)
@@ -285,36 +276,48 @@
         for k in range(0, GROUP, TOGETHER):
             build(GROUP * q + k, TOGETHER)
 
-    def send_group(q):
+    def send_half(q, h):
         for k in range(GROUP):
             if isinstance(q, int) and GROUP * q + k == SELF:
                 continue
-            head_copy(GROUP * q + k, grid).start()
-
-    def build_first(q, carry):
-        build_group(q)
-        return carry
-
-    lax.fori_loop(0, 2, build_first, 0)
+            head_copy(GROUP * q + k, h, grid).start()
+
+    def send_group(q):
+        for h in range(HALVES):
+            send_half(q, h)
+
+    build_group(0)
     pl.semaphore_wait(barrier, GRIDS - 1 + ELEMS - 1)
-    for q in range(FIRST):
-        send_group(q)
+    send_group(0)
 
     def build_next(q, carry):
         build_group(q)
 
-        @pl.when(jnp.logical_and(q % 2 == 0, q >= 4))
+        @pl.when(q < 3)
         def _():
-            send_group(q // 2)
+            send_group(q)
+
+        @pl.when(q == 5)
+        def _():
+            send_group(3)
 
         return carry
 
-    lax.fori_loop(2, GRIDS // GROUP, build_next, 0)
+    lax.fori_loop(1, GRIDS // GROUP, build_next, 0)
 
     guess = dot_t(to_slot.astype(BF16), jnp.where(live, acc_ref[...], 0.0).astype(BF16)).astype(BF16)
     guess_all[elem] = guess
     for k in range(1, ELEMS):
         guess_copy(k, elem).start()
+    pack_row = iota((GRIDS * PACK, 2 * GRIDS), 0)
+    pack_slot = pack_row & (PACK - 1)
+    pack_kind = jnp.where(pack_slot >= 3, 1.0, 0.0)
+    wanted_entry = 2.0 * partner_vector(pack_row >> 4) + pack_kind
+    entry_lane = iota((GRIDS * PACK, 2 * GRIDS), 1).astype(F32)
+    entries = jnp.where(wanted_entry == entry_lane, don_ref[...].astype(F32), 0.0)
+    entry = jnp.sum(entries, axis=1, keepdims=True)
+    used = (iota((GRIDS * PACK, SLOTS), 0) & (PACK - 1)) < 6
+    donor_rows = jnp.where(used, one_hot(entry, SLOTS), 0.0).astype(BF16)
     wide = jnp.concatenate([guess, jnp.zeros((SLOTS, LANES - B), BF16)], axis=1)
     spread = dot(donor_rows, wide)
     row = iota((GRIDS * PACK, 128), 0) & (PACK - 1)
@@ -334,11 +337,13 @@
 
     lax.fori_loop(0, GRIDS, send_tails, 0)
 
-    def send_rest(q, carry):
-        send_group(q)
-        return carry
-
-    lax.fori_loop(EARLY, GRIDS // GROUP, send_rest, 0)
+    for h in range(HALVES):
+
+        def send_rest(q, carry, h=h):
+            send_half(q, h)
+            return carry
+
+        lax.fori_loop(EARLY, GRIDS // GROUP, send_rest, 0)
     own_copy = pltpu.make_async_copy(wire.at[SELF, pl.ds(0, HEAD)], arrived.at[grid, pl.ds(0, HEAD)], own_sem)
     own_copy.start()
 
@@ -419,7 +424,8 @@
     def finish(i, carry):
         @pl.when(i != SELF)
         def _():
-            head_copy(i, sender(i, grid)).wait()
+            for h in range(HALVES):
+                head_copy(i, h, sender(i, grid)).wait()
 
         return carry
 
@@ -473,8 +479,8 @@
             pltpu.SemaphoreType.DMA,
             pltpu.SemaphoreType.DMA,
             pltpu.SemaphoreType.DMA,
-            pltpu.SemaphoreType.DMA((GRIDS,)),
-            pltpu.SemaphoreType.DMA((GRIDS,)),
+            pltpu.SemaphoreType.DMA((GRIDS, HALVES)),
+            pltpu.SemaphoreType.DMA((GRIDS, HALVES)),
             pltpu.SemaphoreType.DMA((ELEMS,)),
             pltpu.SemaphoreType.DMA((ELEMS,)),
             pltpu.SemaphoreType.DMA((GRIDS,)),

time: 102 us -> 95.3 us (0.934)
  Pallas kernels: 101 us -> 94.4 us
    pallas_call x1, Pallas kernels: 95.1 us -> 88.7 us  [shards(): pl.pallas_call(main_kernel, out_shape=(jax.ShapeDtypeStruct((GRIDS, WIRE,...]
where the time goes in v3:
time: 95.3 us; the launch traced here: 95.1 us
  Pallas kernels  94.4 us (99%)
    pallas_call x1, Pallas kernels, shards(): pl.pallas_call(main_kernel, out_shape=(jax.ShapeDtypeStruct((GRIDS, WIRE,...  88.7 us
    pallas_call x1, Pallas kernels, shards(): pl.pallas_call(place_kernel, out_shape=(jax.ShapeDtypeStruct((OWN, B, B),...  5.78 us

profile of v3, /device:TPU:1, one launch (start us, length us, event | category | flops | bytes accessed | tf_op | source)
XLA Modules:
  0.0 95.1 jit_solution(13816184638781606738)
XLA Ops:
  0.6 88.7 %invert_send_sweep.1 = (bf16[32,800,128]{2,1,0:T(8,128)(2,1)}, f32[32,320]{1,0:T(8,128)}) custom-call(bf16[32,320,320]{2,1,0:T(8,128)(2,1)} %jac_hbm.1, bf16[320,1920]{1,0:T(8,128)(2,1)} %fc_hbm.1, s32[32]{0:T(128)} %om1_hbm.1, bf16[32,320]{1,0:T(8,128)(2,1)} %res_hbm.1, s32[1,32]{1,0:T(1,128)} %bitcast.2, s32[6,32]{1,0:T(8,128)} %nb_hbm.1, ...), custom_call_target="tpu_custom_call" | custom-call | tf_op jit(solution)/shard_map/invert_send_sweep/pallas_call | solution.py:449
  89.3 5.8 %place_owned.1 = (bf16[16,320,320]{2,1,0:T(8,128)(2,1)}, f32[32,320]{1,0:T(8,128)}) custom-call(s32[16]{0:T(128)} %owned.1, f32[32,320]{1,0:T(8,128)} %get-tuple-element.4.upd_ref, bf16[32,800,128]{2,1,0:T(8,128)(2,1)} %get-tuple-element.5.w0.w1.w2.w3, bf16[32,800,128]{2,1,0:T(8,128)(2,1)} %get-tuple-element.5.w0.w1.w2.w3, ...), custom_call_target="tpu_custom_call" | custom-call | tf_op jit(solution)/shard_map/place_owned/pallas_call | solution.py:508

commit v4 on v3

--- a/solution.py
+++ b/solution.py
@@ -23,16 +23,16 @@
 WIRE = HEAD + TAIL
 PACK = 16
 HALVES = 2
-SELF = 2
+SELF = 26
 GROUP = 4
 TOGETHER = 4
-EARLY = 4
+EARLY = 5
 LANES = 384
 NODE_PLACES = (-1.0, -0.5, 0.5, 1.0)
 
 
 def offsets(i):
-    step = i // 8
+    step = (i // 8 + 1) % 4
     dc = (i // 4) % 2
     j = i % 4
     dy = (1 + 2 * j - j // 2) % 4
@@ -166,6 +166,8 @@
 ):
     grid = lax.axis_index("grid")
     elem = lax.axis_index("elem")
+    jac_copy = pltpu.make_async_copy(jac_hbm, jac, jac_sem)
+    jac_copy.start()
     barrier = pltpu.get_barrier_semaphore()
     for i in range(GRIDS):
         if i != SELF:
@@ -182,8 +184,6 @@
     small_copies = [pltpu.make_async_copy(a, b, in_sem.at[k]) for k, (a, b) in enumerate(small)]
     for copy in small_copies:
         copy.start()
-    jac_copy = pltpu.make_async_copy(jac_hbm, jac, jac_sem)
-    jac_copy.start()
     fc_copy = pltpu.make_async_copy(fc_hbm, fc, fc_sem)
     fc_copy.start()
 
@@ -223,7 +223,7 @@
     def partner_vector(i):
         j = i & 3
         dy = (1 + 2 * j - (j >> 1)) & 3
-        dz = ((i >> 3) + 4 - dy) & 3
+        dz = ((i >> 3) + 5 - dy) & 3
         dc = (i >> 2) & 1
         c, z, y = grid % 2, (grid // 2) % 4, grid // 8
         return (((y + dy) & 3) * 8 + ((z + dz) & 3) * 2 + ((c + dc) & 1)).astype(F32)
@@ -278,9 +278,13 @@
 
     def send_half(q, h):
         for k in range(GROUP):
-            if isinstance(q, int) and GROUP * q + k == SELF:
+            if k != SELF % GROUP:
+                head_copy(GROUP * q + k, h, grid).start()
                 continue
-            head_copy(GROUP * q + k, h, grid).start()
+
+            @pl.when(q != SELF // GROUP)
+            def _():
+                head_copy(GROUP * q + SELF % GROUP, h, grid).start()
 
     def send_group(q):
         for h in range(HALVES):
@@ -293,13 +297,13 @@
     def build_next(q, carry):
         build_group(q)
 
-        @pl.when(q < 3)
+        @pl.when(q < 4)
         def _():
             send_group(q)
 
-        @pl.when(q == 5)
+        @pl.when(q == 6)
         def _():
-            send_group(3)
+            send_group(4)
 
         return carry
 

time: 95.3 us -> 95 us (level)
  no operation moved by 1% of the time
where the time goes in v4:
time: 95 us; the launch traced here: 94.8 us
  Pallas kernels  94.2 us (99%)
    pallas_call x1, Pallas kernels, shards(): pl.pallas_call(main_kernel, out_shape=(jax.ShapeDtypeStruct((GRIDS, WIRE,...  88.4 us
    pallas_call x1, Pallas kernels, shards(): pl.pallas_call(place_kernel, out_shape=(jax.ShapeDtypeStruct((OWN, B, B),...  5.78 us

profile of v4, /device:TPU:1, one launch (start us, length us, event | category | flops | bytes accessed | tf_op | source)
XLA Modules:
  0.0 94.8 jit_solution(3937605190962083484)
XLA Ops:
  0.6 88.4 %invert_send_sweep.1 = (bf16[32,800,128]{2,1,0:T(8,128)(2,1)}, f32[32,320]{1,0:T(8,128)}) custom-call(bf16[32,320,320]{2,1,0:T(8,128)(2,1)} %jac_hbm.1, bf16[320,1920]{1,0:T(8,128)(2,1)} %fc_hbm.1, s32[32]{0:T(128)} %om1_hbm.1, bf16[32,320]{1,0:T(8,128)(2,1)} %res_hbm.1, s32[1,32]{1,0:T(1,128)} %bitcast.2, s32[6,32]{1,0:T(8,128)} %nb_hbm.1, ...), custom_call_target="tpu_custom_call" | custom-call | tf_op jit(solution)/shard_map/invert_send_sweep/pallas_call | solution.py:453
  89.1 5.8 %place_owned.1 = (bf16[16,320,320]{2,1,0:T(8,128)(2,1)}, f32[32,320]{1,0:T(8,128)}) custom-call(s32[16]{0:T(128)} %owned.1, f32[32,320]{1,0:T(8,128)} %get-tuple-element.4.upd_ref, bf16[32,800,128]{2,1,0:T(8,128)(2,1)} %get-tuple-element.5.w0.w1.w2.w3, bf16[32,800,128]{2,1,0:T(8,128)(2,1)} %get-tuple-element.5.w0.w1.w2.w3, ...), custom_call_target="tpu_custom_call" | custom-call | tf_op jit(solution)/shard_map/place_owned/pallas_call | solution.py:512
